TPU v7x, 32 devices: a whole 2x2x4 slice. The times are simulated.
32 devices in a mesh: row: 4 (over z), col: 8 (over y, x, core).
Axes of the slice: x: 2, y: 2, z: 4, core: 2. Of those that a mesh axis runs over, the one named last changes fastest.
Arguments:
- tokens: bfloat16 [512, 8192], P('col', 'row'), may hold values from -6 to 6
- modality: int32 [512], P('row'), may hold values 0 or 1
- in_weight: bfloat16 [8192, 2, 28672], P('row', None, 'col'), may hold values from -0.0625 to 0.0625
- down_weight: bfloat16 [28672, 8192], P('col', 'row'), may hold values from -0.03125 to 0.03125
- d_mixed: bfloat16 [512, 8192], P('col', 'row'), may hold values from -6 to 6
Outputs:
- mixed: bfloat16 [512, 8192], P('col', 'row')
- d_down: bfloat16 [28672, 8192], P('col', 'row')
- d_in: bfloat16 [8192, 2, 28672], P('row', None, 'col')
- d_tokens: bfloat16 [512, 8192], P('col', 'row')
All inputs are finite; a program needn't handle non-finite values. No bound on the sum of `modality` on one device may be relied on, other than what follows from the above.
Results may differ from a plain program's by a relative error of at most 0.0049.
Values may be sent and summed in bfloat16 or wider, within the bound.
A program may use at most 192 MiB of HBM per device.

v0:
```python
import jax
import jax.numpy as jnp
from jax import lax
from jax.sharding import PartitionSpec as P


def exchange(partial, axis):
    count = lax.axis_size(axis)
    me = lax.axis_index(axis)
    rows = partial.shape[0] // count
    received = []
    for shift in range(1, count):
        start = lax.rem(me + shift, count) * rows
        block = lax.dynamic_slice_in_dim(partial, start, rows, 0).astype(jnp.bfloat16)
        moves = [(i, (i + shift) % count) for i in range(count)]
        received.append(lax.ppermute(block, axis, moves))
    total = lax.dynamic_slice_in_dim(partial, me * rows, rows, 0)
    for block in received:
        total = total + block.astype(jnp.float32)
    return total


def block_terms(rows, cotangents, in_weight, down_weight, spread):
    width = in_weight.shape[2]
    flat_in = in_weight.reshape(in_weight.shape[0], 2 * width)
    d_hidden = exchange(
        jnp.einsum("td,fd->tf", cotangents, down_weight, preferred_element_type=jnp.float32), "row"
    )
    projected = exchange(jnp.dot(rows, flat_in, preferred_element_type=jnp.float32), "row")
    gate_part = projected[:, :width]
    up_part = projected[:, width:]
    sigmoid_gate = jax.nn.sigmoid(gate_part)
    activated = gate_part * sigmoid_gate
    hidden = (activated * up_part).astype(jnp.bfloat16)
    d_gate = d_hidden * up_part * (sigmoid_gate + gate_part * sigmoid_gate * (1.0 - sigmoid_gate))
    d_local = jnp.concatenate([d_gate, d_hidden * activated], 1).astype(jnp.bfloat16)
    hidden_all = lax.all_gather(hidden, "row", axis=0, tiled=True)
    d_projected = lax.all_gather(d_local, "row", axis=0, tiled=True)
    mixed = lax.psum_scatter(
        jnp.dot(spread(hidden_all), down_weight, preferred_element_type=jnp.float32),
        "col",
        scatter_dimension=0,
        tiled=True,
    ).astype(jnp.bfloat16)
    d_down = jnp.einsum(
        "tf,td->fd", hidden_all, cotangents, preferred_element_type=jnp.float32
    ).astype(jnp.bfloat16)
    d_tokens = lax.psum_scatter(
        jnp.einsum("tk,dk->td", spread(d_projected), flat_in, preferred_element_type=jnp.float32),
        "col",
        scatter_dimension=0,
        tiled=True,
    ).astype(jnp.bfloat16)
    d_in = jnp.einsum("td,tk->dk", rows, d_projected, preferred_element_type=jnp.float32)
    d_in = lax.optimization_barrier(d_in.astype(jnp.bfloat16))
    return (mixed, d_down, d_in.reshape(in_weight.shape), d_tokens)


def per_device(tokens, modality, in_weight, down_weight, d_mixed):
    cotangent_all = lax.all_gather(d_mixed, "col", axis=0, tiled=True)
    rows_all = lax.all_gather(tokens, "col", axis=0, tiled=True)
    chosen = lax.all_gather(modality, "row", axis=0, tiled=True) == 1
    total = chosen.shape[0]
    place = jnp.cumsum(chosen.astype(jnp.int32)) - 1
    packed = total * 5 // 8

    def packed_form(rows, cotangents, w_in, w_down):
        pick = (chosen[None, :] & (place[None, :] == jnp.arange(packed)[:, None])).astype(
            jnp.bfloat16
        )
        take = lambda x: jnp.dot(pick, x, preferred_element_type=jnp.float32).astype(jnp.bfloat16)
        spread = lambda x: jnp.einsum(
            "ct,cf->tf", pick, x, preferred_element_type=jnp.float32
        ).astype(jnp.bfloat16)
        return block_terms(take(rows), take(cotangents), w_in, w_down, spread)

    def whole_form(rows, cotangents, w_in, w_down):
        keep = chosen[:, None].astype(jnp.bfloat16)
        return block_terms(rows * keep, cotangents * keep, w_in, w_down, lambda x: x)

    return lax.cond(
        place[-1] < packed, packed_form, whole_form, rows_all, cotangent_all, in_weight, down_weight
    )


def solution(mesh):
    return jax.shard_map(
        per_device,
        mesh=mesh,
        in_specs=(
            P("col", "row"),
            P("row"),
            P("row", None, "col"),
            P("col", "row"),
            P("col", "row"),
        ),
        out_specs=(P("col", "row"), P("col", "row"), P("row", None, "col"), P("col", "row")),
        check_vma=False,
    )
```

profile of v0, /device:TPU:0, one launch (start us, length us, event | category | flops | bytes accessed | tf_op | source)
XLA Modules:
  0.0 546.8 jit_solution(8745290950249474344)
XLA Ops:
  8.7 12.8 %all-gather = s32[4,1,128]{2,1,0:T(1,128)S(1)} all-gather(s32[1,1,128]{2,1,0:T(1,128)} %bitcast.47), channel_id=1, replica_groups=mesh['row'=4,'col'=8] {'row'}, dimensions={0}, use_global_device_ids=true | all-gather | bytes 2560 | tf_op jit(solution)/shard_map/all_gather | solution.py:62
  23.3 17.1 %all-gather.16.cloned.1.call-done = bf16[512,2048]{1,0:T(8,128)(2,1)} async-done(((bf16[64,2048]{1,0:T(8,128)(2,1)}), bf16[512,2048]{1,0:T(8,128)(2,1)}) %all-gather.16.cloned.1.call-update) | async-done | bytes 2097168 | tf_op jit(solution)/shard_map/all_gather | solution.py:61
  40.4 29.7 %all-gather.18.cloned.1.call-done = bf16[512,2048]{1,0:T(8,128)(2,1)} async-done(((bf16[64,2048]{1,0:T(8,128)(2,1)}), bf16[512,2048]{1,0:T(8,128)(2,1)}) %all-gather.18.cloned.1.call-update) | async-done | bytes 2097168 | tf_op jit(solution)/shard_map/all_gather | solution.py:60
  70.1 468.5 %conditional.4 = (bf16[3584,2048]{1,0:T(8,128)(2,1)}, bf16[2048,2,3584]{2,1,0:T(2,128)(2,1)}, bf16[64,2048]{1,0:T(8,128)(2,1)S(1)}, bf16[64,2048]{1,0:T(8,128)(2,1)S(1)}) conditional(s32[]{:T(128)} %bitcast.3, (pred[512]{0:T(512)(128)(4,1)S(1)}, bf16[512,2048]{1,0:T(8,128)(2,1)}, bf16[2048,2,3584]{2,1,0:T(2,128)(2,1)}, bf16[512,2048]{1,0:T(8,128)(2,1)}, ...), branch_computations={%region_2.5_spmd, %region_5.8_spmd} | conditional | flops 67683221504 | bytes 523648416
  77.5 20.9 %copy.10 = bf16[256,8,2,3584]{3,1,2,0:T(8,128)(2,1)} copy(bf16[256,8,2,3584]{3,2,1,0:T(2,128)(2,1)} %bitcast.40) | data formatting | bytes 58720256
  100.3 14.7 %fusion.34 = f32[320,7168]{1,0:T(8,128)S(1)} fusion(bf16[320,2048]{1,0:T(8,128)(2,1)S(1)} %convolution_convert_fusion.5, bf16[2048,7168]{1,0:T(8,128)(2,1)} %bitcast.41), kind=kOutput, calls=%fused_computation.63 | convolution fusion | flops 9395240960 | bytes 39845888 | tf_op jit(solution)/shard_map/cond/branch_1_fun/dot_general | solution.py:29
  115.0 3.6 copy-done
  118.6 1.8 dynamic-slice_convert_fusion.8
  120.4 1.5 collective-permute-start.6
  121.9 2.3 collective-permute-start.8
  124.9 2.0 convolution_convert_fusion.4
  126.8 8.6 %fusion.36 = f32[320,3584]{1,0:T(8,128)S(1)} fusion(bf16[320,2048]{1,0:T(8,128)(2,1)} %convolution_convert_fusion.4, bf16[3584,2048]{1,0:T(8,128)(2,1)} %get-tuple-element.49), kind=kOutput, calls=%fused_computation.65 | convolution fusion | flops 4697620480 | bytes 20578304 | tf_op jit(solution)/shard_map/cond/branch_1_fun/td,fd->tf/dot_general | solution.py:27
  135.4 2.1 copy-done.2
  137.5 1.3 dynamic-slice_convert_fusion.11
  138.8 1.5 collective-permute-start.9
  140.3 2.4 collective-permute-start.11
  142.6 8.1 %collective-permute-done.6 = bf16[80,7168]{1,0:T(8,128)(2,1)} collective-permute-done((bf16[80,7168]{1,0:T(8,128)(2,1)}, bf16[80,7168]{1,0:T(8,128)(2,1)}, u32[]{:S(2)}, u32[]{:S(2)}) %collective-permute-start.6) | collective-permute-done | bytes 1146912 | tf_op jit(solution)/shard_map/cond/branch_1_fun/ppermute | solution.py:16
  150.7 49.7 %collective-permute-start.10 = (bf16[80,3584]{1,0:T(8,128)(2,1)}, bf16[80,3584]{1,0:T(8,128)(2,1)S(1)}, u32[]{:S(2)}, u32[]{:S(2)}) collective-permute-start(bf16[80,3584]{1,0:T(8,128)(2,1)} %get-tuple-element.86), channel_id=1, source_target_pairs={{0,16},{8,24},{16,0},{24,8},{1,17},{9,25},{17,1},{25,9},{2,18},{10... | collective-permute-start | bytes 1720328 | tf_op jit(solution)/shard_map/cond/branch_1_fun/ppermute | solution.py:16
  200.4 47.9 %collective-permute-done.7 = bf16[80,7168]{1,0:T(8,128)(2,1)} collective-permute-done((bf16[80,7168]{1,0:T(8,128)(2,1)S(1)}, bf16[80,7168]{1,0:T(8,128)(2,1)}, u32[]{:S(2)}, u32[]{:S(2)}) %collective-permute-start.7) | collective-permute-done | bytes 1146912 | tf_op jit(solution)/shard_map/cond/branch_1_fun/ppermute | solution.py:16
  248.4 3.2 convert_add_fusion.2
  252.3 20.4 %collective-permute-done.10 = bf16[80,3584]{1,0:T(8,128)(2,1)S(1)} collective-permute-done((bf16[80,3584]{1,0:T(8,128)(2,1)}, bf16[80,3584]{1,0:T(8,128)(2,1)S(1)}, u32[]{:S(2)}, u32[]{:S(2)}) %collective-permute-start.10) | collective-permute-done | bytes 573472 | tf_op jit(solution)/shard_map/cond/branch_1_fun/ppermute | solution.py:16
  272.7 3.0 multiply_convert_fusion.4
  275.8 1.1 pad_maximum_fusion.1
  277.2 45.8 %all-gather.12.cloned.1.call-done = bf16[320,3584]{1,0:T(8,128)(2,1)} async-done(((bf16[80,3584]{1,0:T(8,128)(2,1)}), bf16[320,3584]{1,0:T(8,128)(2,1)}) %all-gather.12.cloned.1.call-update) | async-done | bytes 2293776 | tf_op jit(solution)/shard_map/cond/branch_1_fun/all_gather | solution.py:37
  323.0 17.5 %fusion.11 = f32[512,2048]{1,0:T(8,128)} fusion(bf16[3584,2048]{1,0:T(8,128)(2,1)} %get-tuple-element.49, bf16[320,3584]{1,0:T(8,128)(2,1)} %all-gather.12.cloned.1.call-done, s32[512]{0:T(512)S(1)} %copy-done.9, pred[512]{0:T(512)(128)(4,1)S(1)} %copy-done.7), kind=kOutput, calls=%fused_computation.29 | convolution fusion | flops 8692760576 | bytes 21170688 | tf_op jit(solution)/shard_map/cond/branch_1_fun/dot_general | solution.py:40
  340.8 70.2 %all-gather.14.cloned.1.call-done = bf16[320,7168]{1,0:T(8,128)(2,1)} async-done(((bf16[80,7168]{1,0:T(8,128)(2,1)}), bf16[320,7168]{1,0:T(8,128)(2,1)}) %all-gather.14.cloned.1.call-update) | async-done | bytes 4587536 | tf_op jit(solution)/shard_map/cond/branch_1_fun/all_gather | solution.py:38
  411.0 6.6 %convolution_convert_fusion.2.clone.4 = bf16[512,7168]{1,0:T(8,128)(2,1)S(1)} fusion(bf16[320,7168]{1,0:T(8,128)(2,1)} %all-gather.14.cloned.1.call-done, s32[512]{0:T(512)S(1)} %copy-done.9, pred[512]{0:T(512)(128)(4,1)S(1)} %copy-done.7), kind=kOutput, calls=%fused_computation.27.clone.clone.clone.1 | convolution fusion | flops 2352807936 | bytes 11930112 | tf_op jit(solution)/shard_map/cond/branch_1_fun/ct,cf->tf/dot_general | solution.py:72
  417.6 22.0 %fusion.12 = f32[512,2048]{1,0:T(8,128)} fusion(bf16[2048,7168]{1,0:T(8,128)(2,1)} %bitcast.42, bf16[512,7168]{1,0:T(8,128)(2,1)S(1)} %convolution_convert_fusion.2.clone.4), kind=kOutput, calls=%fused_computation.36 | convolution fusion | flops 15032385536 | bytes 40894464 | tf_op jit(solution)/shard_map/cond/branch_1_fun/tk,dk->td/dot_general | solution.py:49
  439.6 1.6 copy-done.10
  441.3 12.6 %fusion.35 = bf16[3584,2048]{1,0:T(8,128)(2,1)} fusion(bf16[320,3584]{1,0:T(8,128)(2,1)S(1)} %copy-done.10, bf16[320,2048]{1,0:T(8,128)(2,1)} %convolution_convert_fusion.4), kind=kOutput, calls=%fused_computation.64 | convolution fusion | flops 4697620480 | bytes 18284544 | tf_op jit(solution)/shard_map/cond/branch_1_fun/tf,td->fd/dot_general | solution.py:45
  453.9 19.5 %convolution_convert_fusion.1 = bf16[2048,7168]{1,0:T(8,128)(2,1)} fusion(bf16[320,2048]{1,0:T(8,128)(2,1)S(1)} %copy-done.17, bf16[320,7168]{1,0:T(8,128)(2,1)S(1)} %bitcast.49), kind=kOutput, calls=%fused_computation.26 | convolution fusion | flops 9409921024 | bytes 35258368 | tf_op jit(solution)/shard_map/cond/branch_1_fun/td,tk->dk/dot_general | solution.py:54
  473.4 62.7 %reshape.42 = bf16[2048,2,3584]{2,1,0:T(2,128)(2,1)} reshape(bf16[2048,7168]{1,0:T(8,128)(2,1)} %convolution_convert_fusion.1) | data formatting | bytes 58720256 | tf_op jit(solution)/shard_map/cond/branch_1_fun/reshape | solution.py:56
  (59 shorter events, 9.7 us)
Async XLA Ops:
  7.2 33.2 %all-gather.16.cloned.1.call-start = ((), (), s32[]{:S(2)}) async-start(), calls=%async_computation.12 | async-start | bytes 2359296 | tf_op jit(solution)/shard_map/all_gather | solution.py:61
  7.9 62.2 %all-gather.18.cloned.1.call-start = ((), (), s32[]{:S(2)}) async-start(), calls=%async_computation.13 | async-start | bytes 2359296 | tf_op jit(solution)/shard_map/all_gather | solution.py:60
  77.4 47.5 %copy-start.6 = (pred[512]{0:T(512)(128)(4,1)}, pred[512]{0:T(512)(128)(4,1)S(1)}, u32[]{:S(2)}) copy-start(pred[512]{0:T(512)(128)(4,1)S(1)} %get-tuple-element.44) | copy-start | bytes 1540
  77.4 47.5 %copy-start.8 = (s32[512]{0:T(512)}, s32[512]{0:T(512)S(1)}, u32[]{:S(2)}) copy-start(s32[512]{0:T(512)S(1)} %get-tuple-element.45) | copy-start | bytes 6148
  77.4 245.6 %all-gather.12.cloned.1.call-start = ((), (), s32[]{:S(2)}) async-start(), calls=%async_computation.8 | async-start | bytes 2867200 | tf_op jit(solution)/shard_map/cond/branch_1_fun/all_gather | solution.py:37
  77.5 20.9 %copy-start.13 = (bf16[512,2048]{1,0:T(8,128)(2,1)S(1)}, bf16[512,2048]{1,0:T(8,128)(2,1)}, u32[]{:S(2)}) copy-start(bf16[512,2048]{1,0:T(8,128)(2,1)} %get-tuple-element.46) | copy-start | bytes 6291460
  99.2 1.1 copy-start.16
  115.0 3.7 copy-start
  118.6 6.2 %copy-start.15 = (bf16[512,2048]{1,0:T(8,128)(2,1)S(1)}, bf16[512,2048]{1,0:T(8,128)(2,1)}, u32[]{:S(2)}) copy-start(bf16[512,2048]{1,0:T(8,128)(2,1)} %get-tuple-element.48) | copy-start | bytes 6291460
  120.4 30.3 %collective-permute-start.6 = (bf16[80,7168]{1,0:T(8,128)(2,1)}, bf16[80,7168]{1,0:T(8,128)(2,1)}, u32[]{:S(2)}, u32[]{:S(2)}) collective-permute-start(bf16[80,7168]{1,0:T(8,128)(2,1)} %get-tuple-element.79), channel_id=1, source_target_pairs={{0,8},{8,16},{16,24},{24,0},{1,9},{9,17},{17,25},{25,1},{2,10},{10... | collective-permute-start | bytes 3440648 | tf_op jit(solution)/shard_map/cond/branch_1_fun/ppermute | solution.py:16
  121.9 78.5 %collective-permute-start.8 = (bf16[80,7168]{1,0:T(8,128)(2,1)}, bf16[80,7168]{1,0:T(8,128)(2,1)}, u32[]{:S(2)}, u32[]{:S(2)}) collective-permute-start(bf16[80,7168]{1,0:T(8,128)(2,1)} %get-tuple-element.80), channel_id=1, source_target_pairs={{0,24},{8,0},{16,8},{24,16},{1,25},{9,1},{17,9},{25,17},{2,26},{10... | collective-permute-start | bytes 3440648 | tf_op jit(solution)/shard_map/cond/branch_1_fun/ppermute | solution.py:16
  124.3 124.1 %collective-permute-start.7 = (bf16[80,7168]{1,0:T(8,128)(2,1)S(1)}, bf16[80,7168]{1,0:T(8,128)(2,1)}, u32[]{:S(2)}, u32[]{:S(2)}) collective-permute-start(bf16[80,7168]{1,0:T(8,128)(2,1)S(1)} %get-tuple-element.81), channel_id=1, source_target_pairs={{0,16},{8,24},{16,0},{24,8},{1,17},{9,25},{17,1},{25,9},{2,18},{10... | collective-permute-start | bytes 3440648 | tf_op jit(solution)/shard_map/cond/branch_1_fun/ppermute | solution.py:16
  135.4 2.1 copy-start.2
  138.8 112.7 %collective-permute-start.9 = (bf16[80,3584]{1,0:T(8,128)(2,1)}, bf16[80,3584]{1,0:T(8,128)(2,1)S(1)}, u32[]{:S(2)}, u32[]{:S(2)}) collective-permute-start(bf16[80,3584]{1,0:T(8,128)(2,1)} %get-tuple-element.84), channel_id=1, source_target_pairs={{0,8},{8,16},{16,24},{24,0},{1,9},{9,17},{17,25},{25,1},{2,10},{10... | collective-permute-start | bytes 1720328 | tf_op jit(solution)/shard_map/cond/branch_1_fun/ppermute | solution.py:16
  140.3 111.3 %collective-permute-start.11 = (bf16[80,3584]{1,0:T(8,128)(2,1)}, bf16[80,3584]{1,0:T(8,128)(2,1)S(1)}, u32[]{:S(2)}, u32[]{:S(2)}) collective-permute-start(bf16[80,3584]{1,0:T(8,128)(2,1)} %get-tuple-element.85), channel_id=1, source_target_pairs={{0,24},{8,0},{16,8},{24,16},{1,25},{9,1},{17,9},{25,17},{2,26},{10... | collective-permute-start | bytes 1720328 | tf_op jit(solution)/shard_map/cond/branch_1_fun/ppermute | solution.py:16
  150.7 122.0 %collective-permute-start.10 = (bf16[80,3584]{1,0:T(8,128)(2,1)}, bf16[80,3584]{1,0:T(8,128)(2,1)S(1)}, u32[]{:S(2)}, u32[]{:S(2)}) collective-permute-start(bf16[80,3584]{1,0:T(8,128)(2,1)} %get-tuple-element.86), channel_id=1, source_target_pairs={{0,16},{8,24},{16,0},{24,8},{1,17},{9,25},{17,1},{25,9},{2,18},{10... | collective-permute-start | bytes 1720328 | tf_op jit(solution)/shard_map/cond/branch_1_fun/ppermute | solution.py:16
  251.5 0.8 copy-start.3
  275.7 47.3 %copy-start.7 = (pred[512]{0:T(512)(128)(4,1)S(1)}, pred[512]{0:T(512)(128)(4,1)}, u32[]{:S(2)}) copy-start(pred[512]{0:T(512)(128)(4,1)} %copy-done.6) | copy-start | bytes 1540
  275.7 47.3 %copy-start.9 = (s32[512]{0:T(512)S(1)}, s32[512]{0:T(512)}, u32[]{:S(2)}) copy-start(s32[512]{0:T(512)} %copy-done.8) | copy-start | bytes 6148
  275.8 135.3 %all-gather.14.cloned.1.call-start = ((), (), s32[]{:S(2)}) async-start(), calls=%async_computation.9 | async-start | bytes 5734400 | tf_op jit(solution)/shard_map/cond/branch_1_fun/all_gather | solution.py:38
  276.9 259.1 %reduce-scatter.9.cloned.1.call-start = ((), (), s32[]{:S(2)}) async-start(), calls=%async_computation.10 | async-start | bytes 4718592 | tf_op jit(solution)/shard_map/cond/branch_1_fun/reduce_scatter | solution.py:39
  340.5 196.6 %reduce-scatter.11.cloned.1.call-start = ((), (), s32[]{:S(2)}) async-start(), calls=%async_computation.11 | async-start | bytes 4718592 | tf_op jit(solution)/shard_map/cond/branch_1_fun/reduce_scatter | solution.py:48
  439.6 1.6 copy-start.10
  439.6 14.2 %slice-start = ((s8[4587520]{0:T(1024)(128)(4,1)}), s8[393216]{0:T(1024)(128)(4,1)S(1)}, s32[]{:S(2)}) async-start(s8[4587520]{0:T(1024)(128)(4,1)} %bitcast.48), calls=%async_computation.14 | async-start | bytes 786432
  441.3 12.6 %slice-start.1 = ((s8[4587520]{0:T(1024)(128)(4,1)}), s8[4194304]{0:T(1024)(128)(4,1)S(1)}, s32[]{:S(2)}) async-start(s8[4587520]{0:T(1024)(128)(4,1)} %bitcast.48), calls=%async_computation.15 | async-start | bytes 8388608
  441.3 12.6 %copy-start.17 = (bf16[320,2048]{1,0:T(8,128)(2,1)S(1)}, bf16[320,2048]{1,0:T(8,128)(2,1)}, u32[]{:S(2)}) copy-start(bf16[320,2048]{1,0:T(8,128)(2,1)} %copy-done.16) | copy-start | bytes 3932164
  538.6 0.7 copy-start.4
  538.6 0.8 copy-start.5
Sparse Core Ops, SparseCore 0:
  9.9 30.4 all-gather.15
  42.3 27.7 all-gather.17
  275.9 47.0 all-gather.11
  325.0 85.9 all-gather.13
  414.2 49.5 reduce-scatter.8
  467.1 51.1 reduce-scatter.10
where the time goes:
time: 557 us; the launch traced here: 547 us
  waiting for transfers between devices  241 us (43%)
  matrix products  104 us (19%)
  local copies, waits for them, and re-layouts  97.4 us (17%)
  starting transfers between devices  58.7 us (11%)
  between operations  15.3 us (3%)
  blocking collectives  12.8 us (2%)
  other arithmetic  9.84 us (2%)
  loops' own time  7.87 us (1%)
    ppermute x6, waiting for transfers between devices, exchange(): received.append(lax.ppermute(block, axis, moves))  76.4 us
    all_gather x1, waiting for transfers between devices, block_terms(): d_projected = lax.all_gather(d_local, 'row', axis=0, tiled=True)  70.2 us
    reshape x1, local copies, waits for them, and re-layouts, block_terms(): return (mixed, d_down, d_in.reshape(in_weight.shape), d_tokens)  62.7 us
    ppermute x6, starting transfers between devices, exchange(): received.append(lax.ppermute(block, axis, moves))  58 us
    all_gather x1, waiting for transfers between devices, block_terms(): hidden_all = lax.all_gather(hidden, 'row', axis=0, tiled=True)  45.8 us
    unnamed x33, local copies, waits for them, and re-layouts  30.9 us
    all_gather x1, waiting for transfers between devices, per_device(): cotangent_all = lax.all_gather(d_mixed, 'col', axis=0, tiled=True)  29.7 us
    dot_general x1, matrix products, block_terms(): jnp.einsum('tk,dk->td', spread(d_projected), flat_in, preferred_element_t...  22 us
  transfers between devices with their start and end apart: 12, of which 7 were waited for; matrix products, arithmetic and copies ran while one was open for 29% of the time, Pallas kernels for 0%

commit v1 on v0

--- a/solution.py
+++ b/solution.py
@@ -34,7 +34,14 @@
     hidden = (activated * up_part).astype(jnp.bfloat16)
     d_gate = d_hidden * up_part * (sigmoid_gate + gate_part * sigmoid_gate * (1.0 - sigmoid_gate))
     d_local = jnp.concatenate([d_gate, d_hidden * activated], 1).astype(jnp.bfloat16)
-    hidden_all = lax.all_gather(hidden, "row", axis=0, tiled=True)
+    size = lax.axis_size("row")
+    right = [(i_2, (i_2 + 1) % size) for i_2 in range(size)]
+    terms = [hidden]
+    for far in range(1, size):
+        terms = [lax.ppermute(terms[0], "row", right), *terms]
+    out = jnp.concatenate(terms, axis=0)
+    offset = (lax.axis_index("row") + 1) * terms[-1].shape[0]
+    hidden_all = jnp.roll(out, offset, axis=0)
     d_projected = lax.all_gather(d_local, "row", axis=0, tiled=True)
     mixed = lax.psum_scatter(
         jnp.dot(spread(hidden_all), down_weight, preferred_element_type=jnp.float32),

time: 557 us -> 536 us (0.962)
  waiting for transfers between devices: 241 us -> 218 us
    ppermute x0 -> x3, waiting for transfers between devices: none -> 62 us  [block_terms(): terms = [lax.ppermute(terms[0], 'row', right), *terms]]
    all_gather x1 -> x0, waiting for transfers between devices: 45.8 us -> none  [block_terms(): hidden_all = lax.all_gather(hidden, 'row', axis=0, tiled=True)]
    all_gather x1, waiting for transfers between devices: 70.2 us -> 30.9 us  [block_terms(): d_projected = lax.all_gather(d_local, 'row', axis=0, tiled=True)]
    unnamed x33 -> x40, local copies, waits for them, and re-layouts: 30.9 us -> 33.1 us
  transfers between devices with their start and end apart: 12 -> 14, of which waited for: 7 -> 9; matrix products, arithmetic and copies ran while one was open for 29% -> 32% of each run, Pallas kernels for 0% -> 0%
where the time goes in v1:
time: 536 us; the launch traced here: 527 us
  waiting for transfers between devices  218 us (41%)
  matrix products  104 us (19%)
  local copies, waits for them, and re-layouts  100 us (19%)
  starting transfers between devices  58.7 us (11%)
  between operations  16.4 us (3%)
  blocking collectives  12.8 us (2%)
  other arithmetic  9 us (2%)
  loops' own time  8.07 us (2%)
    ppermute x6, waiting for transfers between devices, exchange(): received.append(lax.ppermute(block, axis, moves))  76.5 us
    reshape x1, local copies, waits for them, and re-layouts, block_terms(): return (mixed, d_down, d_in.reshape(in_weight.shape), d_tokens)  62.5 us
    ppermute x3, waiting for transfers between devices, block_terms(): terms = [lax.ppermute(terms[0], 'row', right), *terms]  62 us
    ppermute x6, starting transfers between devices, exchange(): received.append(lax.ppermute(block, axis, moves))  58 us
    unnamed x40, local copies, waits for them, and re-layouts  33.1 us
    all_gather x1, waiting for transfers between devices, block_terms(): d_projected = lax.all_gather(d_local, 'row', axis=0, tiled=True)  30.9 us
    all_gather x1, waiting for transfers between devices, per_device(): cotangent_all = lax.all_gather(d_mixed, 'col', axis=0, tiled=True)  29.7 us
    dot_general x1, matrix products, block_terms(): jnp.einsum('tk,dk->td', spread(d_projected), flat_in, preferred_element_t...  21.6 us
  transfers between devices with their start and end apart: 14, of which 9 were waited for; matrix products, arithmetic and copies ran while one was open for 32% of the time, Pallas kernels for 0%

profile of v1, /device:TPU:0, one launch (start us, length us, event | category | flops | bytes accessed | tf_op | source)
XLA Modules:
  0.0 527.2 jit_solution(18251095467633059480)
XLA Ops:
  9.5 12.8 %all-gather = s32[4,1,128]{2,1,0:T(1,128)S(1)} all-gather(s32[1,1,128]{2,1,0:T(1,128)} %bitcast.43), channel_id=1, replica_groups=mesh['row'=4,'col'=8] {'row'}, dimensions={0}, use_global_device_ids=true | all-gather | bytes 2560 | tf_op jit(solution)/shard_map/all_gather | solution.py:69
  24.2 17.1 %all-gather.10.cloned.1.call-done = bf16[512,2048]{1,0:T(8,128)(2,1)} async-done(((bf16[64,2048]{1,0:T(8,128)(2,1)}), bf16[512,2048]{1,0:T(8,128)(2,1)}) %all-gather.10.cloned.1.call-update) | async-done | bytes 2097168 | tf_op jit(solution)/shard_map/all_gather | solution.py:68
  41.2 29.7 %all-gather.12.cloned.1.call-done = bf16[512,2048]{1,0:T(8,128)(2,1)} async-done(((bf16[64,2048]{1,0:T(8,128)(2,1)}), bf16[512,2048]{1,0:T(8,128)(2,1)}) %all-gather.12.cloned.1.call-update) | async-done | bytes 2097168 | tf_op jit(solution)/shard_map/all_gather | solution.py:67
  70.9 447.8 %conditional.4 = (bf16[3584,2048]{1,0:T(8,128)(2,1)}, bf16[2048,2,3584]{2,1,0:T(2,128)(2,1)}, bf16[64,2048]{1,0:T(8,128)(2,1)S(1)}, bf16[64,2048]{1,0:T(8,128)(2,1)S(1)}) conditional(s32[]{:T(128)} %bitcast.3, (pred[512]{0:T(512)(128)(4,1)S(1)}, bf16[512,2048]{1,0:T(8,128)(2,1)}, bf16[2048,2,3584]{2,1,0:T(2,128)(2,1)}, bf16[512,2048]{1,0:T(8,128)(2,1)}, ...), branch_computations={%region_2.5_spmd, %region_5.8_spmd} | conditional | flops 67683221504 | bytes 554441344
  78.5 20.9 %copy.10 = bf16[256,8,2,3584]{3,1,2,0:T(8,128)(2,1)} copy(bf16[256,8,2,3584]{3,2,1,0:T(2,128)(2,1)} %bitcast.36) | data formatting | bytes 58720256
  101.3 14.7 %fusion.45 = f32[320,7168]{1,0:T(8,128)S(1)} fusion(bf16[320,2048]{1,0:T(8,128)(2,1)S(1)} %convolution_convert_fusion.5, bf16[2048,7168]{1,0:T(8,128)(2,1)} %bitcast.39), kind=kOutput, calls=%fused_computation.88 | convolution fusion | flops 9395240960 | bytes 39845888 | tf_op jit(solution)/shard_map/cond/branch_1_fun/dot_general | solution.py:29
  116.0 1.8 dynamic-slice_convert_fusion.8
  117.8 1.5 collective-permute-start.9
  119.3 2.3 collective-permute-start.11
  122.2 1.9 convolution_convert_fusion.4
  124.2 8.6 %fusion.46 = f32[320,3584]{1,0:T(8,128)S(1)} fusion(bf16[320,2048]{1,0:T(8,128)(2,1)} %convolution_convert_fusion.4, bf16[3584,2048]{1,0:T(8,128)(2,1)} %get-tuple-element.49), kind=kOutput, calls=%fused_computation.89 | convolution fusion | flops 4697620480 | bytes 20578304 | tf_op jit(solution)/shard_map/cond/branch_1_fun/td,fd->tf/dot_general | solution.py:27
  132.8 2.1 copy-done.2
  134.9 1.2 dynamic-slice_convert_fusion.11
  136.0 1.5 collective-permute-start.15
  137.5 2.3 collective-permute-start.17
  139.9 8.2 %collective-permute-done.9 = bf16[80,7168]{1,0:T(8,128)(2,1)} collective-permute-done((bf16[80,7168]{1,0:T(8,128)(2,1)}, bf16[80,7168]{1,0:T(8,128)(2,1)}, u32[]{:S(2)}, u32[]{:S(2)}) %collective-permute-start.9) | collective-permute-done | bytes 1146912 | tf_op jit(solution)/shard_map/cond/branch_1_fun/ppermute | solution.py:16
  148.1 49.7 %collective-permute-start.16 = (bf16[80,3584]{1,0:T(8,128)(2,1)S(1)}, bf16[80,3584]{1,0:T(8,128)(2,1)S(1)}, u32[]{:S(2)}, u32[]{:S(2)}) collective-permute-start(bf16[80,3584]{1,0:T(8,128)(2,1)S(1)} %get-tuple-element.86), channel_id=1, source_target_pairs={{0,16},{8,24},{16,0},{24,8},{1,17},{9,25},{17,1},{25,9},{2,18},{10... | collective-permute-start | bytes 1720328 | tf_op jit(solution)/shard_map/cond/branch_1_fun/ppermute | solution.py:16
  197.8 47.9 %collective-permute-done.10 = bf16[80,7168]{1,0:T(8,128)(2,1)} collective-permute-done((bf16[80,7168]{1,0:T(8,128)(2,1)S(1)}, bf16[80,7168]{1,0:T(8,128)(2,1)}, u32[]{:S(2)}, u32[]{:S(2)}) %collective-permute-start.10) | collective-permute-done | bytes 1146912 | tf_op jit(solution)/shard_map/cond/branch_1_fun/ppermute | solution.py:16
  245.7 3.2 convert_add_fusion.2
  249.7 20.4 %collective-permute-done.16 = bf16[80,3584]{1,0:T(8,128)(2,1)S(1)} collective-permute-done((bf16[80,3584]{1,0:T(8,128)(2,1)S(1)}, bf16[80,3584]{1,0:T(8,128)(2,1)S(1)}, u32[]{:S(2)}, u32[]{:S(2)}) %collective-permute-start.16) | collective-permute-done | bytes 573472 | tf_op jit(solution)/shard_map/cond/branch_1_fun/ppermute | solution.py:16
  270.1 2.2 multiply_convert_fusion.4
  272.3 16.7 %collective-permute-done.12 = bf16[80,3584]{1,0:T(8,128)(2,1)S(1)} collective-permute-done((bf16[80,3584]{1,0:T(8,128)(2,1)S(1)}, bf16[80,3584]{1,0:T(8,128)(2,1)S(1)}, u32[]{:S(2)}, u32[]{:S(2)}) %collective-permute-start.12) | collective-permute-done | bytes 573472 | tf_op jit(solution)/shard_map/cond/branch_1_fun/ppermute | solution.py:41
  290.2 17.0 %collective-permute-done.13 = bf16[80,3584]{1,0:T(8,128)(2,1)S(1)} collective-permute-done((bf16[80,3584]{1,0:T(8,128)(2,1)S(1)}, bf16[80,3584]{1,0:T(8,128)(2,1)S(1)}, u32[]{:S(2)}, u32[]{:S(2)}) %collective-permute-start.13) | collective-permute-done | bytes 573472 | tf_op jit(solution)/shard_map/cond/branch_1_fun/ppermute | solution.py:41
  307.4 28.3 %collective-permute-done.14 = bf16[80,3584]{1,0:T(8,128)(2,1)S(1)} collective-permute-done((bf16[80,3584]{1,0:T(8,128)(2,1)S(1)}, bf16[80,3584]{1,0:T(8,128)(2,1)S(1)}, u32[]{:S(2)}, u32[]{:S(2)}) %collective-permute-start.14) | collective-permute-done | bytes 573472 | tf_op jit(solution)/shard_map/cond/branch_1_fun/ppermute | solution.py:41
  342.7 17.7 %fusion.16 = f32[512,2048]{1,0:T(8,128)} fusion(bf16[3584,2048]{1,0:T(8,128)(2,1)} %get-tuple-element.49, bf16[640,3584]{1,0:T(8,128)(2,1)} %constant_dynamic-update-slice_fusion.8, s32[]{:T(128)S(6)} %select_n.54, s32[512]{0:T(512)S(1)} %copy-done.10, pred[512]{0:T(512)(128)(4,1)S(1)} %copy-done.8), kind=kOutput, calls=%fused_computation.42 | convolution fusion | flops 8692760576 | bytes 21170692 | tf_op jit(solution)/shard_map/cond/branch_1_fun/dot_general | solution.py:47
  360.7 30.9 %all-gather.8.cloned.1.call-done = bf16[320,7168]{1,0:T(8,128)(2,1)} async-done(((bf16[80,7168]{1,0:T(8,128)(2,1)}), bf16[320,7168]{1,0:T(8,128)(2,1)}) %all-gather.8.cloned.1.call-update) | async-done | bytes 4587536 | tf_op jit(solution)/shard_map/cond/branch_1_fun/all_gather | solution.py:45
  391.6 6.6 %convolution_convert_fusion.2.clone.4 = bf16[512,7168]{1,0:T(8,128)(2,1)S(1)} fusion(bf16[320,7168]{1,0:T(8,128)(2,1)} %all-gather.8.cloned.1.call-done, s32[512]{0:T(512)S(1)} %copy-done.10, pred[512]{0:T(512)(128)(4,1)S(1)} %copy-done.8), kind=kOutput, calls=%fused_computation.40.clone.clone.clone.1 | convolution fusion | flops 2352807936 | bytes 11930112 | tf_op jit(solution)/shard_map/cond/branch_1_fun/ct,cf->tf/dot_general | solution.py:79
  398.2 21.6 %fusion.21 = f32[512,2048]{1,0:T(8,128)} fusion(bf16[2048,7168]{1,0:T(8,128)(2,1)} %bitcast.40, bf16[512,7168]{1,0:T(8,128)(2,1)S(1)} %convolution_convert_fusion.2.clone.4), kind=kOutput, calls=%fused_computation.52 | convolution fusion | flops 15032385536 | bytes 40894464 | tf_op jit(solution)/shard_map/cond/branch_1_fun/tk,dk->td/dot_general | solution.py:56
  419.8 1.3 copy-done.18
  421.1 13.2 %fusion.19 = bf16[3584,2048]{1,0:T(8,128)(2,1)} fusion(bf16[320,2048]{1,0:T(8,128)(2,1)S(1)} %copy-done.18, bf16[640,3584]{1,0:T(8,128)(2,1)} %constant_dynamic-update-slice_fusion.8, s32[]{:T(128)S(6)} %select_n.54), kind=kOutput, calls=%fused_computation.50 | convolution fusion | flops 4697620480 | bytes 18284548 | tf_op jit(solution)/shard_map/cond/branch_1_fun/tf,td->fd/dot_general | solution.py:52
  434.2 19.5 %convolution_convert_fusion.1 = bf16[2048,7168]{1,0:T(8,128)(2,1)} fusion(bf16[320,2048]{1,0:T(8,128)(2,1)S(1)} %copy-done.17, bf16[320,7168]{1,0:T(8,128)(2,1)S(1)} %bitcast.45), kind=kOutput, calls=%fused_computation.39 | convolution fusion | flops 9409921024 | bytes 35258368 | tf_op jit(solution)/shard_map/cond/branch_1_fun/td,tk->dk/dot_general | solution.py:61
  453.7 62.5 %reshape.42 = bf16[2048,2,3584]{2,1,0:T(2,128)(2,1)} reshape(bf16[2048,7168]{1,0:T(8,128)(2,1)} %convolution_convert_fusion.1) | data formatting | bytes 58720256 | tf_op jit(solution)/shard_map/cond/branch_1_fun/reshape | solution.py:63
  (70 shorter events, 17.8 us)
Async XLA Ops:
  8.0 33.2 %all-gather.10.cloned.1.call-start = ((), (), s32[]{:S(2)}) async-start(), calls=%async_computation.10 | async-start | bytes 2359296 | tf_op jit(solution)/shard_map/all_gather | solution.py:68
  8.7 62.2 %all-gather.12.cloned.1.call-start = ((), (), s32[]{:S(2)}) async-start(), calls=%async_computation.11 | async-start | bytes 2359296 | tf_op jit(solution)/shard_map/all_gather | solution.py:67
  78.4 43.8 %copy-start.7 = (pred[512]{0:T(512)(128)(4,1)}, pred[512]{0:T(512)(128)(4,1)S(1)}, u32[]{:S(2)}) copy-start(pred[512]{0:T(512)(128)(4,1)S(1)} %get-tuple-element.44) | copy-start | bytes 1540
  78.4 43.8 %copy-start.9 = (s32[512]{0:T(512)}, s32[512]{0:T(512)S(1)}, u32[]{:S(2)}) copy-start(s32[512]{0:T(512)S(1)} %get-tuple-element.45) | copy-start | bytes 6148
  78.4 313.2 %all-gather.8.cloned.1.call-start = ((), (), s32[]{:S(2)}) async-start(), calls=%async_computation.7 | async-start | bytes 5734400 | tf_op jit(solution)/shard_map/cond/branch_1_fun/all_gather | solution.py:45
  78.5 20.9 %copy-start.13 = (bf16[512,2048]{1,0:T(8,128)(2,1)S(1)}, bf16[512,2048]{1,0:T(8,128)(2,1)}, u32[]{:S(2)}) copy-start(bf16[512,2048]{1,0:T(8,128)(2,1)} %get-tuple-element.46) | copy-start | bytes 6291460
  100.2 1.1 copy-start.16
  116.0 8.2 %copy-start = (f32[320,7168]{1,0:T(8,128)}, f32[320,7168]{1,0:T(8,128)S(1)}, u32[]{:S(2)}) copy-start(f32[320,7168]{1,0:T(8,128)S(1)} %fusion.45) | copy-start | bytes 27525124
  116.0 6.2 %copy-start.15 = (bf16[512,2048]{1,0:T(8,128)(2,1)S(1)}, bf16[512,2048]{1,0:T(8,128)(2,1)}, u32[]{:S(2)}) copy-start(bf16[512,2048]{1,0:T(8,128)(2,1)} %get-tuple-element.48) | copy-start | bytes 6291460
  117.8 30.3 %collective-permute-start.9 = (bf16[80,7168]{1,0:T(8,128)(2,1)}, bf16[80,7168]{1,0:T(8,128)(2,1)}, u32[]{:S(2)}, u32[]{:S(2)}) collective-permute-start(bf16[80,7168]{1,0:T(8,128)(2,1)} %get-tuple-element.79), channel_id=1, source_target_pairs={{0,8},{8,16},{16,24},{24,0},{1,9},{9,17},{17,25},{25,1},{2,10},{10... | collective-permute-start | bytes 3440648 | tf_op jit(solution)/shard_map/cond/branch_1_fun/ppermute | solution.py:16
  119.3 78.5 %collective-permute-start.11 = (bf16[80,7168]{1,0:T(8,128)(2,1)}, bf16[80,7168]{1,0:T(8,128)(2,1)}, u32[]{:S(2)}, u32[]{:S(2)}) collective-permute-start(bf16[80,7168]{1,0:T(8,128)(2,1)} %get-tuple-element.80), channel_id=1, source_target_pairs={{0,24},{8,0},{16,8},{24,16},{1,25},{9,1},{17,9},{25,17},{2,26},{10... | collective-permute-start | bytes 3440648 | tf_op jit(solution)/shard_map/cond/branch_1_fun/ppermute | solution.py:16
  121.6 124.1 %collective-permute-start.10 = (bf16[80,7168]{1,0:T(8,128)(2,1)S(1)}, bf16[80,7168]{1,0:T(8,128)(2,1)}, u32[]{:S(2)}, u32[]{:S(2)}) collective-permute-start(bf16[80,7168]{1,0:T(8,128)(2,1)S(1)} %get-tuple-element.81), channel_id=1, source_target_pairs={{0,16},{8,24},{16,0},{24,8},{1,17},{9,25},{17,1},{25,9},{2,18},{10... | collective-permute-start | bytes 3440648 | tf_op jit(solution)/shard_map/cond/branch_1_fun/ppermute | solution.py:16
  132.8 2.1 copy-start.2
  136.0 112.8 %collective-permute-start.15 = (bf16[80,3584]{1,0:T(8,128)(2,1)}, bf16[80,3584]{1,0:T(8,128)(2,1)S(1)}, u32[]{:S(2)}, u32[]{:S(2)}) collective-permute-start(bf16[80,3584]{1,0:T(8,128)(2,1)} %get-tuple-element.84), channel_id=1, source_target_pairs={{0,8},{8,16},{16,24},{24,0},{1,9},{9,17},{17,25},{25,1},{2,10},{10... | collective-permute-start | bytes 1720328 | tf_op jit(solution)/shard_map/cond/branch_1_fun/ppermute | solution.py:16
  137.5 111.3 %collective-permute-start.17 = (bf16[80,3584]{1,0:T(8,128)(2,1)}, bf16[80,3584]{1,0:T(8,128)(2,1)S(1)}, u32[]{:S(2)}, u32[]{:S(2)}) collective-permute-start(bf16[80,3584]{1,0:T(8,128)(2,1)} %get-tuple-element.85), channel_id=1, source_target_pairs={{0,24},{8,0},{16,8},{24,16},{1,25},{9,1},{17,9},{25,17},{2,26},{10... | collective-permute-start | bytes 1720328 | tf_op jit(solution)/shard_map/cond/branch_1_fun/ppermute | solution.py:16
  148.1 122.0 %collective-permute-start.16 = (bf16[80,3584]{1,0:T(8,128)(2,1)S(1)}, bf16[80,3584]{1,0:T(8,128)(2,1)S(1)}, u32[]{:S(2)}, u32[]{:S(2)}) collective-permute-start(bf16[80,3584]{1,0:T(8,128)(2,1)S(1)} %get-tuple-element.86), channel_id=1, source_target_pairs={{0,16},{8,24},{16,0},{24,8},{1,17},{9,25},{17,1},{25,9},{2,18},{10... | collective-permute-start | bytes 1720328 | tf_op jit(solution)/shard_map/cond/branch_1_fun/ppermute | solution.py:16
  248.9 0.8 copy-start.3
  272.2 16.7 %collective-permute-start.12 = (bf16[80,3584]{1,0:T(8,128)(2,1)S(1)}, bf16[80,3584]{1,0:T(8,128)(2,1)S(1)}, u32[]{:S(2)}, u32[]{:S(2)}) collective-permute-start(bf16[80,3584]{1,0:T(8,128)(2,1)S(1)} %get-tuple-element.87), channel_id=1, source_target_pairs={{0,8},{8,16},{16,24},{24,0},{1,9},{9,17},{17,25},{25,1},{2,10},{10... | collective-permute-start | bytes 1720328 | tf_op jit(solution)/shard_map/cond/branch_1_fun/ppermute | solution.py:41
  289.0 18.2 %collective-permute-start.13 = (bf16[80,3584]{1,0:T(8,128)(2,1)S(1)}, bf16[80,3584]{1,0:T(8,128)(2,1)S(1)}, u32[]{:S(2)}, u32[]{:S(2)}) collective-permute-start(bf16[80,3584]{1,0:T(8,128)(2,1)S(1)} %collective-permute-done.12), channel_id=1, source_target_pairs={{0,8},{8,16},{16,24},{24,0},{1,9},{9,17},{17,25},{25,1},{2,10},{10... | collective-permute-start | bytes 1720328 | tf_op jit(solution)/shard_map/cond/branch_1_fun/ppermute | solution.py:41
  290.1 226.1 %reduce-scatter.9.cloned.1.call-start = ((), (), s32[]{:S(2)}) async-start(), calls=%async_computation.8 | async-start | bytes 4718592 | tf_op jit(solution)/shard_map/cond/branch_1_fun/reduce_scatter | solution.py:46
  307.2 28.5 %collective-permute-start.14 = (bf16[80,3584]{1,0:T(8,128)(2,1)S(1)}, bf16[80,3584]{1,0:T(8,128)(2,1)S(1)}, u32[]{:S(2)}, u32[]{:S(2)}) collective-permute-start(bf16[80,3584]{1,0:T(8,128)(2,1)S(1)} %collective-permute-done.13), channel_id=1, source_target_pairs={{0,8},{8,16},{16,24},{24,0},{1,9},{9,17},{17,25},{25,1},{2,10},{10... | collective-permute-start | bytes 1720328 | tf_op jit(solution)/shard_map/cond/branch_1_fun/ppermute | solution.py:41
  337.4 5.2 copy-start.8
  337.5 5.2 copy-start.10
  360.4 156.9 %reduce-scatter.11.cloned.1.call-start = ((), (), s32[]{:S(2)}) async-start(), calls=%async_computation.9 | async-start | bytes 4718592 | tf_op jit(solution)/shard_map/cond/branch_1_fun/reduce_scatter | solution.py:55
  419.7 1.3 copy-start.18
  419.7 14.5 %slice-start = ((s8[4587520]{0:T(1024)(128)(4,1)}), s8[393216]{0:T(1024)(128)(4,1)S(1)}, s32[]{:S(2)}) async-start(s8[4587520]{0:T(1024)(128)(4,1)} %bitcast.44), calls=%async_computation.12 | async-start | bytes 786432
  421.1 13.2 %slice-start.1 = ((s8[4587520]{0:T(1024)(128)(4,1)}), s8[4194304]{0:T(1024)(128)(4,1)S(1)}, s32[]{:S(2)}) async-start(s8[4587520]{0:T(1024)(128)(4,1)} %bitcast.44), calls=%async_computation.13 | async-start | bytes 8388608
  421.1 13.2 %copy-start.17 = (bf16[320,2048]{1,0:T(8,128)(2,1)S(1)}, bf16[320,2048]{1,0:T(8,128)(2,1)}, u32[]{:S(2)}) copy-start(bf16[320,2048]{1,0:T(8,128)(2,1)} %copy-done.16) | copy-start | bytes 3932164
  518.7 0.7 copy-start.4
  518.7 0.8 copy-start.5
Sparse Core Ops, SparseCore 0:
  10.7 30.4 all-gather.9
  43.1 27.7 all-gather.11
  290.2 101.3 all-gather.7
Sparse Core Ops, SparseCore 1:
  360.5 59.4 reduce-scatter.8
  423.1 51.0 reduce-scatter.10
